TPU v7x, 32 devices: a whole 2x2x4 slice. The times are simulated.
32 devices in a mesh: seq: 16 (over z, x, core), fsdp: 2 (over y).
Axes of the slice: x: 2, y: 2, z: 4, core: 2. Of those that a mesh axis runs over, the one named last changes fastest.
Arguments:
- activations: bfloat16 [65536, 2048], P('seq', 'fsdp'), may hold values from -3 to 3
- mix_first: bfloat16 [256, 256], replicated, may hold values from -0.375 to 0.375
- twiddle: float32 [256, 256], P('seq'), may hold values from 0.4 to 2
- mix_second: bfloat16 [256, 256], replicated, may hold values from -0.375 to 0.375
- up_first: bfloat16 [8, 256, 256], P('fsdp'), may hold values from -0.375 to 0.375
- up_second: bfloat16 [8, 256, 1024], P('fsdp'), may hold values from -0.375 to 0.375
- down_first: bfloat16 [8, 1024, 256], P('fsdp'), may hold values from -0.1875 to 0.1875
- down_second: bfloat16 [8, 256, 256], P('fsdp'), may hold values from -0.375 to 0.375
- grad_out: bfloat16 [65536, 2048], P('seq', 'fsdp'), may hold values from -3 to 3
Outputs:
- output: bfloat16 [65536, 2048], P('seq', 'fsdp')
- grad_inputs: bfloat16 [65536, 2048], P('seq', 'fsdp')
- grad_up_first: float32 [8, 256, 256], P('fsdp')
- grad_up_second: float32 [8, 256, 1024], P('fsdp')
- grad_down_first: float32 [8, 1024, 256], P('fsdp')
- grad_down_second: float32 [8, 256, 256], P('fsdp')
All inputs are finite; a program needn't handle non-finite values.
Results may differ from a plain program's by a relative error of at most 0.01.
Values may be sent and summed in bfloat16 or wider, within the bound.
No kernel may reach another device: no remote copies, remote signals or barrier semaphores. Data moves between devices by JAX's collectives and lax.ppermute only.
A program may use at most 320 MiB of HBM per device.

v0:
```python
import jax
import jax.numpy as jnp
from jax import lax
from jax.sharding import PartitionSpec as P

NBLK = 8
root_two_pi = 0.7978845608028654
cubic_term = 0.044715


def gelu_value(values):
    inner = root_two_pi * (values + cubic_term * values * values * values)
    return 0.5 * values * (1.0 + jnp.tanh(inner))


def gelu_slope(values):
    inner = root_two_pi * (values + cubic_term * values * values * values)
    hyper = jnp.tanh(inner)
    return 0.5 * (1.0 + hyper) + 0.5 * values * (1.0 - hyper * hyper) * root_two_pi * (
        1.0 + 3.0 * cubic_term * values * values
    )


def product(form, left, right):
    return jnp.einsum(form, left, right, preferred_element_type=jnp.float32)


def column_pass(field, factor):
    result = product(
        "ajc,ai->ijc", lax.all_to_all(field, "seq", split_axis=1, concat_axis=0, tiled=True), factor
    ).astype(jnp.bfloat16)
    return lax.all_to_all(result, "seq", split_axis=0, concat_axis=1, tiled=True)


def shuffle_blocks(values):
    return lax.all_to_all(values, "fsdp", split_axis=2, concat_axis=1, tiled=True)


def spread_blocks(values):
    count, local_blocks, width = values.shape
    stride = width // NBLK
    received = shuffle_blocks(values)
    shaped = received.reshape(count, NBLK, local_blocks, stride)
    return jnp.transpose(shaped, (0, 2, 3, 1)).reshape(count, local_blocks, width)


def return_blocks(values):
    count, local_blocks, width = values.shape
    stride = width // NBLK
    parts = NBLK // local_blocks
    shaped = values.reshape(count, local_blocks, stride, parts, local_blocks)
    sending = jnp.transpose(shaped, (0, 1, 3, 4, 2)).reshape(count, local_blocks, width)
    received = shuffle_blocks(sending).reshape(count, NBLK, local_blocks, stride)
    return jnp.transpose(received, (0, 2, 1, 3)).reshape(count, local_blocks, width)


def blocks_layer(hidden, grad_out, up_first, up_second, down_first, down_second):
    count, channels = hidden.shape
    local_blocks, width = (up_first.shape[0], up_first.shape[1])
    hidden_three = hidden.reshape(count, local_blocks, width)
    up_mid = product("tkp,kpq->tkq", hidden_three, up_first).astype(jnp.bfloat16)
    up_perm = spread_blocks(up_mid)
    pre_act = product("tge,geo->tgo", up_perm, up_second)
    activated = gelu_value(pre_act).astype(jnp.bfloat16)
    down_mid = product("tgo,goq->tgq", activated, down_first).astype(jnp.bfloat16)
    down_perm = spread_blocks(down_mid)
    down_out = product("tge,geq->tgq", down_perm, down_second).reshape(count, channels)
    output = (hidden.astype(jnp.float32) + down_out).astype(jnp.bfloat16)
    grad_three = grad_out.reshape(count, local_blocks, width)
    sum_down_second = product("tge,tgq->geq", down_perm, grad_three)
    back_perm = product("tgq,geq->tge", grad_three, down_second).astype(jnp.bfloat16)
    back_mid = return_blocks(back_perm)
    sum_down_first = product("tgo,tgq->goq", activated, back_mid)
    grad_act = product("tgq,goq->tgo", back_mid, down_first)
    grad_pre = (grad_act * gelu_slope(pre_act)).astype(jnp.bfloat16)
    sum_up_second = product("tge,tgo->geo", up_perm, grad_pre)
    grad_perm = product("tgo,geo->tge", grad_pre, up_second).astype(jnp.bfloat16)
    grad_mid = return_blocks(grad_perm)
    sum_up_first = product("tkp,tkq->kpq", hidden_three, grad_mid)
    grad_inner = product("tkq,kpq->tkp", grad_mid, up_first).reshape(count, channels)
    grad_hidden = (grad_out.astype(jnp.float32) + grad_inner).astype(jnp.bfloat16)
    return (output, grad_hidden, (sum_up_first, sum_up_second, sum_down_first, sum_down_second))


def shards(
    activations,
    mix_first,
    twiddle,
    mix_second,
    up_first,
    up_second,
    down_first,
    down_second,
    grad_out,
):
    local_rows, local_channels = activations.shape
    block_rows = twiddle.shape[0]
    length = mix_first.shape[0]
    inputs_three = activations.reshape(block_rows, length, local_channels)
    first_pass = (product("abc,bj->ajc", inputs_three, mix_first) * twiddle[:, :, None]).astype(
        jnp.bfloat16
    )
    mixed = column_pass(first_pass, mix_second).reshape(local_rows, local_channels)
    inputs_float = activations.astype(jnp.float32)
    gating = jax.nn.sigmoid(inputs_float)
    mixed_float = mixed.astype(jnp.float32)
    hidden = (inputs_float + gating * mixed_float).astype(jnp.bfloat16)
    output, grad_hidden, grads = blocks_layer(
        hidden, grad_out, up_first, up_second, down_first, down_second
    )
    totals = lax.psum((grads[0], grads[1], grads[2], grads[3]), "seq")
    grad_float = grad_hidden.astype(jnp.float32)
    grad_mixed = (grad_float * gating).astype(jnp.bfloat16)
    back_rows = column_pass(grad_mixed.reshape(block_rows, length, local_channels), mix_second.T)
    twisted = (back_rows.astype(jnp.float32) * twiddle[:, :, None]).astype(jnp.bfloat16)
    mix_grad = product("ajc,bj->abc", twisted, mix_first).reshape(local_rows, local_channels)
    grad_inputs = (grad_float * (1.0 + gating * (1.0 - gating) * mixed_float) + mix_grad).astype(
        jnp.bfloat16
    )
    scale = 1.0 / length
    return (
        output,
        grad_inputs,
        totals[0] * scale,
        totals[1] * scale,
        totals[2] * scale,
        totals[3] * scale,
    )


def solution(mesh):
    in_specs = (
        P("seq", "fsdp"),
        P(),
        P("seq", None),
        P(),
        P("fsdp", None, None),
        P("fsdp", None, None),
        P("fsdp", None, None),
        P("fsdp", None, None),
        P("seq", "fsdp"),
    )
    out_specs = (
        P("seq", "fsdp"),
        P("seq", "fsdp"),
        P("fsdp", None, None),
        P("fsdp", None, None),
        P("fsdp", None, None),
        P("fsdp", None, None),
    )
    return jax.shard_map(shards, mesh=mesh, in_specs=in_specs, out_specs=out_specs, check_vma=False)
```

profile of v0, /device:TPU:0, one launch (start us, length us, event | category | flops | bytes accessed | tf_op | source)
XLA Modules:
  0.0 1738.0 jit_solution(1957139552533190147)
XLA Ops:
  28.0 189.5 %all_to_all.114 = bf16[16,256,1024]{2,0,1:T(8,128)(2,1)} all-to-all(bf16[16,256,1024]{2,0,1:T(8,128)(2,1)} %copy.130), channel_id=1, replica_groups=mesh['seq'=16,'fsdp'=2] {'seq'}, dimensions={1} | all-to-all | bytes 16777216 | tf_op jit(solution)/shard_map/all_to_all | solution.py:30
  230.3 17.0 convert_bitcast_fusion.7
  311.6 104.5 %all-to-all-done.1 = bf16[256,16,1024]{2,1,0:T(8,128)(2,1)} async-done(((bf16[256,16,1024]{2,1,0:T(8,128)(2,1)}), bf16[256,16,1024]{2,1,0:T(8,128)(2,1)}, u32[]{:S(2)}, u32[]{:S(2)}) %all-to-all-start.1) | async-done | bytes 8388640 | tf_op jit(solution)/shard_map/all_to_all | solution.py:32
  492.7 24.1 %all-to-all-done.4 = bf16[4096,4,256]{0,1,2:T(4,128)(2,1)} async-done(((bf16[4096,4,256]{0,1,2:T(4,128)(2,1)}), bf16[4096,4,256]{0,1,2:T(4,128)(2,1)}, u32[]{:S(2)}, u32[]{:S(2)}) %all-to-all-start.4) | async-done | bytes 8388640 | tf_op jit(solution)/shard_map/all_to_all | solution.py:36
  550.8 66.1 %all-to-all-done.2 = bf16[4096,4,256]{0,1,2:T(4,128)(2,1)} async-done(((bf16[4096,4,256]{0,1,2:T(4,128)(2,1)}), bf16[4096,4,256]{0,1,2:T(4,128)(2,1)}, u32[]{:S(2)}, u32[]{:S(2)}) %all-to-all-start.2) | async-done | bytes 8388640 | tf_op jit(solution)/shard_map/all_to_all | solution.py:36
  635.9 48.6 %multiply_convert_fusion = (bf16[4096,4,1024]{2,0,1:T(8,128)(2,1)}, f32[4,4096,1024]{2,1,0:T(8,128)}) fusion(bf16[4,256,1024]{2,1,0:T(8,128)(2,1)S(1)} %copy-done, bf16[4096,4,32,8]{0,2,1,3:T(8,128)(2,1)} %bitcast.185), kind=kOutput, calls=%fused_computation.10 | convolution fusion | flops 8740929536 | bytes 111149056 | tf_op jit(solution)/shard_map/tge,geo->tgo/dot_general | solution.py:25
  684.5 53.2 %fusion.6 = bf16[4096,4,1024]{2,0,1:T(8,128)(2,1)} fusion(f32[4,4096,1024]{2,1,0:T(8,128)} %get-tuple-element.11, bf16[4096,4,256]{0,2,1:T(8,128)(2,1)} %bitcast.183, bf16[4,1024,256]{2,1,0:T(8,128)(2,1)} %param.15), kind=kOutput, calls=%fused_computation.8 | convolution fusion | flops 8908701696 | bytes 111149056 | tf_op jit(solution)/shard_map/tgq,goq->tgo/dot_general | solution.py:25
  737.7 19.0 %convert_bitcast_fusion.3 = bf16[4096,4,256]{0,2,1:T(8,128)(2,1)} fusion(bf16[4096,4,1024]{2,0,1:T(8,128)(2,1)} %fusion.6, bf16[4,256,1024]{2,1,0:T(8,128)(2,1)S(1)} %copy-done), kind=kOutput, calls=%fused_computation.50 | convolution fusion | flops 8594128896 | bytes 44040192 | tf_op jit(solution)/shard_map/tgo,geo->tge/dot_general | solution.py:25
  791.4 96.6 %all_to_all.115 = bf16[4096,4,256]{0,1,2:T(4,128)(2,1)} all-to-all(bf16[4096,4,256]{0,1,2:T(4,128)(2,1)S(1)} %copy.157), channel_id=1, replica_groups=mesh['seq'=16,'fsdp'=2] {'fsdp'}, dimensions={2} | all-to-all | bytes 16777216 | tf_op jit(solution)/shard_map/all_to_all | solution.py:36
  926.3 17.4 %copy.162 = f32[4096,1024]{1,0:T(8,128)} copy(f32[4096,1024]{0,1:T(8,128)} %bitcast.164) | data formatting | bytes 33554432 | tf_op jit(solution)/shard_map/reshape | solution.py:80
  943.8 15.4 fusion.13
  970.5 35.0 %all-to-all-start.6 = ((bf16[16,256,1024]{2,0,1:T(8,128)(2,1)}), bf16[16,256,1024]{2,0,1:T(8,128)(2,1)}, u32[]{:S(2)}, u32[]{:S(2)}) async-start(bf16[16,256,1024]{2,0,1:T(8,128)(2,1)} %copy.163), calls=%async_computation.6 | async-start | bytes 16777216 | tf_op jit(solution)/shard_map/all_to_all | solution.py:30
  1005.5 17.1 convert_bitcast_fusion.5
  1022.6 14.6 copy.142
  1037.2 118.8 %all-to-all-done.6 = bf16[16,256,1024]{2,0,1:T(8,128)(2,1)} async-done(((bf16[16,256,1024]{2,0,1:T(8,128)(2,1)}), bf16[16,256,1024]{2,0,1:T(8,128)(2,1)}, u32[]{:S(2)}, u32[]{:S(2)}) %all-to-all-start.6) | async-done | bytes 8388640 | tf_op jit(solution)/shard_map/all_to_all | solution.py:30
  1176.0 23.3 %convert_bitcast_fusion.2 = bf16[256,16,1024]{0,2,1:T(8,128)(2,1)} fusion(bf16[256,16,1024]{2,1,0:T(8,128)(2,1)} %bitcast.162, bf16[256,256]{1,0:T(8,128)(2,1)S(1)} %copy-done.10), kind=kOutput, calls=%fused_computation.49 | convolution fusion | flops 2151677952 | bytes 16908288 | tf_op jit(solution)/shard_map/ajc,ai->ijc/dot_general | solution.py:25
  1211.7 45.2 %all-to-all-done.3 = bf16[4096,4,256]{0,1,2:T(4,128)(2,1)} async-done(((bf16[4096,4,256]{0,1,2:T(4,128)(2,1)}), bf16[4096,4,256]{0,1,2:T(4,128)(2,1)}, u32[]{:S(2)}, u32[]{:S(2)}) %all-to-all-start.3) | async-done | bytes 8388640 | tf_op jit(solution)/shard_map/all_to_all | solution.py:36
  1256.9 36.0 %all-to-all-start.7 = ((bf16[256,16,1024]{2,1,0:T(8,128)(2,1)}), bf16[256,16,1024]{2,1,0:T(8,128)(2,1)}, u32[]{:S(2)}, u32[]{:S(2)}) async-start(bf16[256,16,1024]{2,1,0:T(8,128)(2,1)} %copy.167), calls=%async_computation.7 | async-start | bytes 16777216 | tf_op jit(solution)/shard_map/all_to_all | solution.py:32
  1293.3 20.5 %fusion.51 = f32[4,1024,256]{2,1,0:T(8,128)} fusion(bf16[4096,4,1024]{2,0,1:T(8,128)(2,1)} %get-tuple-element.10, bf16[4096,4,256]{0,2,1:T(8,128)(2,1)} %bitcast.184), kind=kOutput, calls=%fused_computation.71 | convolution fusion | flops 8589934592 | bytes 46137344 | tf_op jit(solution)/shard_map/tgo,tgq->goq/dot_general | solution.py:25
  1313.9 26.3 %fusion.25 = f32[4,256,1024]{2,1,0:T(8,128)} fusion(bf16[4096,4,1024]{2,0,1:T(8,128)(2,1)} %fusion.6, bf16[4096,4,32,8]{0,2,1,3:T(8,128)(2,1)} %bitcast.186), kind=kOutput, calls=%fused_computation.41 | convolution fusion | flops 8589934592 | bytes 46137344 | tf_op jit(solution)/shard_map/tge,tgo->geo/dot_general | solution.py:25
  1379.6 15.1 fusion.23
  1394.7 17.5 %copy.148 = f32[4096,1024]{1,0:T(8,128)} copy(f32[4096,1024]{0,1:T(8,128)} %bitcast.163) | data formatting | bytes 33554432 | tf_op jit(solution)/shard_map/reshape | solution.py:67
  1424.3 243.4 %all-reduce.3.cloned.1.call-done = (f32[4,256,256]{2,1,0:T(8,128)}, f32[4,256,1024]{2,1,0:T(8,128)}, f32[4,1024,256]{2,1,0:T(8,128)}, f32[4,256,256]{2,1,0:T(8,128)}) async-done(((f32[4,256,256]{2,1,0:T(8,128)}, f32[4,256,1024]{2,1,0:T(8,128)}, f32[4,1024,256]{2,1,0:T(8,128)}, f32[4,256,256]{2,1,0:T(8,128)}), (f32[4,256,256]{2,1,0:T(8,128)}, f32[4,256,1024]{2,1,0:T(8,128)}, f32[4,1024,256]{2,1,0:T(8,128)}, ...) | async-done | bytes 10485776 | tf_op jit(solution)/shard_map/psum | solution.py:111
  1707.0 23.6 %fusion.12 = bf16[4096,1024]{1,0:T(8,128)(2,1)} fusion(f32[16,1024,256]{1,2,0:T(8,128)} %fusion.47, f32[16,16,16,1024]{3,2,1,0:T(8,128)} %copy-done.2, bf16[4096,1024]{1,0:T(8,128)(2,1)S(1)} %bitcast.159, f32[4096,1024]{1,0:T(8,128)} %copy.162, bf16[4096,1024]{1,0:T(8,128)(2,1)} %param.17), kind=kLoop, calls=%fused_computation.21 | loop fusion | flops 62914560 | bytes 75497472 | tf_op jit(solution)/shard_map/convert_element_type | solution.py:117
  (89 shorter events, 435.3 us)
Async XLA Ops:
  7.2 628.7 %copy-start = (bf16[4,256,1024]{2,1,0:T(8,128)(2,1)S(1)}, bf16[4,256,1024]{2,1,0:T(8,128)(2,1)}, u32[]{:S(2)}) copy-start(bf16[4,256,1024]{2,1,0:T(8,128)(2,1)} %param.14) | copy-start | bytes 6291460
  217.4 12.9 copy-start.9
  259.6 5.9 copy-start.6
  259.6 156.5 %all-to-all-start.1 = ((bf16[256,16,1024]{2,1,0:T(8,128)(2,1)}), bf16[256,16,1024]{2,1,0:T(8,128)(2,1)}, u32[]{:S(2)}, u32[]{:S(2)}) async-start(bf16[256,16,1024]{2,1,0:T(8,128)(2,1)} %copy.134), calls=%async_computation.1 | async-start | bytes 16777216 | tf_op jit(solution)/shard_map/all_to_all | solution.py:32
  416.1 100.7 %all-to-all-start.4 = ((bf16[4096,4,256]{0,1,2:T(4,128)(2,1)}), bf16[4096,4,256]{0,1,2:T(4,128)(2,1)}, u32[]{:S(2)}, u32[]{:S(2)}) async-start(bf16[4096,4,256]{0,1,2:T(4,128)(2,1)} %copy.151), calls=%async_computation.4 | async-start | bytes 16777216 | tf_op jit(solution)/shard_map/all_to_all | solution.py:36
  423.0 24.6 %slice-start = ((s8[8388608]{0:T(1024)(128)(4,1)}), s8[4194304]{0:T(1024)(128)(4,1)S(1)}, s32[]{:S(2)}) async-start(s8[8388608]{0:T(1024)(128)(4,1)} %bitcast.156), calls=%async_computation.9 | async-start | bytes 8388608
  434.6 13.0 slice-start.1
  441.9 5.8 copy-start.2
  456.3 12.0 copy-start.4
  516.8 100.1 %all-to-all-start.2 = ((bf16[4096,4,256]{0,1,2:T(4,128)(2,1)}), bf16[4096,4,256]{0,1,2:T(4,128)(2,1)}, u32[]{:S(2)}, u32[]{:S(2)}) async-start(bf16[4096,4,256]{0,1,2:T(4,128)(2,1)} %copy.137), calls=%async_computation.2 | async-start | bytes 16777216 | tf_op jit(solution)/shard_map/all_to_all | solution.py:36
  907.0 7.8 copy-start.5
  970.5 35.0 %copy-start.12 = (bf16[4,1024,256]{2,1,0:T(8,128)(2,1)S(1)}, bf16[4,1024,256]{2,1,0:T(8,128)(2,1)}, u32[]{:S(2)}) copy-start(bf16[4,1024,256]{2,1,0:T(8,128)(2,1)} %param.15) | copy-start | bytes 6291460
  970.5 185.5 %all-to-all-start.6 = ((bf16[16,256,1024]{2,0,1:T(8,128)(2,1)}), bf16[16,256,1024]{2,0,1:T(8,128)(2,1)}, u32[]{:S(2)}, u32[]{:S(2)}) async-start(bf16[16,256,1024]{2,0,1:T(8,128)(2,1)} %copy.163), calls=%async_computation.6 | async-start | bytes 16777216 | tf_op jit(solution)/shard_map/all_to_all | solution.py:30
  1156.0 100.9 %all-to-all-start.3 = ((bf16[4096,4,256]{0,1,2:T(4,128)(2,1)}), bf16[4096,4,256]{0,1,2:T(4,128)(2,1)}, u32[]{:S(2)}, u32[]{:S(2)}) async-start(bf16[4096,4,256]{0,1,2:T(4,128)(2,1)} %copy.142), calls=%async_computation.3 | async-start | bytes 16777216 | tf_op jit(solution)/shard_map/all_to_all | solution.py:36
  1163.2 12.8 copy-start.10
  1256.9 421.4 %all-to-all-start.7 = ((bf16[256,16,1024]{2,1,0:T(8,128)(2,1)}), bf16[256,16,1024]{2,1,0:T(8,128)(2,1)}, u32[]{:S(2)}, u32[]{:S(2)}) async-start(bf16[256,16,1024]{2,1,0:T(8,128)(2,1)} %copy.167), calls=%async_computation.7 | async-start | bytes 16777216 | tf_op jit(solution)/shard_map/all_to_all | solution.py:32
  1292.9 374.7 %all-reduce.3.cloned.1.call-start = ((), (), s32[]{:S(2)}) async-start(), calls=%async_computation.8 | async-start | bytes 20971520 | tf_op jit(solution)/shard_map/psum | solution.py:111
  1351.5 20.1 %slice-start.4 = ((s8[8388608]{0:T(1024)(128)(4,1)}), s8[4194304]{0:T(1024)(128)(4,1)S(1)}, s32[]{:S(2)}) async-start(s8[8388608]{0:T(1024)(128)(4,1)} %bitcast.166), calls=%async_computation.13 | async-start | bytes 8388608
  1359.3 12.3 slice-start.5
  1667.6 8.3 copy-start.3
  1689.7 6.6 copy-start.11
  1696.3 10.7 slice-start.2
  1698.9 8.1 slice-start.3
  1707.0 23.6 %copy-start.1 = (bf16[4,256,1024]{2,1,0:T(8,128)(2,1)S(1)}, bf16[4,256,1024]{2,1,0:T(8,128)(2,1)}, u32[]{:S(2)}) copy-start(bf16[4,256,1024]{2,1,0:T(8,128)(2,1)} %param.14) | copy-start | bytes 6291460
  (2 other events, 3.7 us)
Sparse Core Ops, SparseCore 0:
  1378.7 288.8 all-reduce.2
where the time goes:
time: 1750 us; the launch traced here: 1740 us
  waiting for transfers between devices  602 us (34%)
  local copies, waits for them, and re-layouts  333 us (19%)
  matrix products  307 us (18%)
  blocking collectives  286 us (16%)
  starting transfers between devices  98.6 us (6%)
  other arithmetic  95.9 us (5%)
    dot_general x16, matrix products, product(): return jnp.einsum(form, left, right, preferred_element_type=jnp.float32)  307 us
    psum x1, waiting for transfers between devices, shards(): totals = lax.psum((grads[0], grads[1], grads[2], grads[3]), 'seq')  243 us
    all_to_all x1, blocking collectives, column_pass(): lax.all_to_all(field, 'seq', split_axis=1, concat_axis=0, tiled=True)  189 us
    all_to_all x3, waiting for transfers between devices, shuffle_blocks(): lax.all_to_all(values, 'fsdp', split_axis=2, concat_axis=1, tiled=True)  135 us
    all_to_all x1, waiting for transfers between devices, column_pass(): lax.all_to_all(field, 'seq', split_axis=1, concat_axis=0, tiled=True)  119 us
    all_to_all x2, waiting for transfers between devices, column_pass(): lax.all_to_all(result, 'seq', split_axis=0, concat_axis=1, tiled=True)  104 us
    all_to_all x1, blocking collectives, shuffle_blocks(): lax.all_to_all(values, 'fsdp', split_axis=2, concat_axis=1, tiled=True)  96.6 us
    all_to_all x8, local copies, waits for them, and re-layouts, shuffle_blocks(): lax.all_to_all(values, 'fsdp', split_axis=2, concat_axis=1, tiled=True)  76.1 us
  transfers between devices with their start and end apart: 7, of which 6 were waited for; matrix products, arithmetic and copies ran while one was open for 21% of the time, Pallas kernels for 0%

commit v1 on v0

--- a/solution.py
+++ b/solution.py
@@ -33,7 +33,10 @@
 
 
 def shuffle_blocks(values):
-    return lax.all_to_all(values, "fsdp", split_axis=2, concat_axis=1, tiled=True)
+    return jnp.concatenate(
+        lax.all_to_all(jnp.stack(jnp.split(values, lax.axis_size("fsdp"), axis=2)), "fsdp", 0, 0),
+        axis=1,
+    )
 
 
 def spread_blocks(values):

time: 1750 us -> 1730 us (0.989)
  local copies, waits for them, and re-layouts: 333 us -> 250 us
  waiting for transfers between devices: 602 us -> 634 us
  other arithmetic: 95.9 us -> 120 us
    all_to_all x8 -> x0, local copies, waits for them, and re-layouts: 76.1 us -> none  [shuffle_blocks(): lax.all_to_all(values, 'fsdp', split_axis=2, concat_axis=1, tiled=True)]
    convert_element_type x2 -> x0, local copies, waits for them, and re-layouts: 29.2 us -> none  [the longest x1 14.6 us: blocks_layer(): product('tgo,goq->tgq', activated, down_first).astype(jnp.bfloat16)]
    another operation x0 -> x4, other arithmetic: none -> 24.8 us  [shuffle_blocks(): jnp.stack(jnp.split(values, lax.axis_size('fsdp'), axis=2))]
    all_to_all x3, waiting for transfers between devices: 135 us -> 158 us  [shuffle_blocks(): lax.all_to_all(jnp.stack(jnp.split(values, lax.axis_size('fsdp'), axis=2)...]
    another operation x0 -> x4, local copies, waits for them, and re-layouts: none -> 20.4 us  [shuffle_blocks(): jnp.stack(jnp.split(values, lax.axis_size('fsdp'), axis=2))]
  transfers between devices with their start and end apart: 7 -> 7, of which waited for: 6 -> 6; matrix products, arithmetic and copies ran while one was open for 21% -> 19% of each run, Pallas kernels for 0% -> 0%
where the time goes in v1:
time: 1730 us; the launch traced here: 1720 us
  waiting for transfers between devices  634 us (37%)
  matrix products  309 us (18%)
  blocking collectives  293 us (17%)
  local copies, waits for them, and re-layouts  250 us (14%)
  other arithmetic  120 us (7%)
  starting transfers between devices  98.4 us (6%)
    dot_general x16, matrix products, product(): return jnp.einsum(form, left, right, preferred_element_type=jnp.float32)  309 us
    psum x1, waiting for transfers between devices, shards(): totals = lax.psum((grads[0], grads[1], grads[2], grads[3]), 'seq')  249 us
    all_to_all x1, blocking collectives, column_pass(): lax.all_to_all(field, 'seq', split_axis=1, concat_axis=0, tiled=True)  189 us
    all_to_all x3, waiting for transfers between devices, shuffle_blocks(): lax.all_to_all(jnp.stack(jnp.split(values, lax.axis_size('fsdp'), axis=2)...  158 us
    all_to_all x1, waiting for transfers between devices, column_pass(): lax.all_to_all(field, 'seq', split_axis=1, concat_axis=0, tiled=True)  122 us
    all_to_all x2, waiting for transfers between devices, column_pass(): lax.all_to_all(result, 'seq', split_axis=0, concat_axis=1, tiled=True)  105 us
    all_to_all x1, blocking collectives, shuffle_blocks(): lax.all_to_all(jnp.stack(jnp.split(values, lax.axis_size('fsdp'), axis=2)...  103 us
    reshape x4, local copies, waits for them, and re-layouts, return_blocks(): shaped = values.reshape(count, local_blocks, stride, parts, local_blocks)  49.3 us
  transfers between devices with their start and end apart: 7, of which 6 were waited for; matrix products, arithmetic and copies ran while one was open for 19% of the time, Pallas kernels for 0%

profile of v1, /device:TPU:0, one launch (start us, length us, event | category | flops | bytes accessed | tf_op | source)
XLA Modules:
  0.0 1718.8 jit_solution(11657792446542434405)
XLA Ops:
  28.0 189.5 %all_to_all.74 = bf16[16,256,1024]{2,0,1:T(8,128)(2,1)} all-to-all(bf16[16,256,1024]{2,0,1:T(8,128)(2,1)} %copy.126), channel_id=1, replica_groups=mesh['seq'=16,'fsdp'=2] {'seq'}, dimensions={1} | all-to-all | bytes 16777216 | tf_op jit(solution)/shard_map/all_to_all | solution.py:30
  230.3 16.8 convert_bitcast_fusion.7
  274.4 13.1 reshape.88
  310.5 105.3 %all-to-all-done.1 = bf16[256,16,1024]{2,1,0:T(8,128)(2,1)} async-done(((bf16[256,16,1024]{2,1,0:T(8,128)(2,1)}), bf16[256,16,1024]{2,1,0:T(8,128)(2,1)}, u32[]{:S(2)}, u32[]{:S(2)}) %all-to-all-start.1) | async-done | bytes 8388640 | tf_op jit(solution)/shard_map/all_to_all | solution.py:32
  489.2 27.3 %all-to-all-done.4 = bf16[2,4096,4,128]{1,3,2,0:T(8,128)(2,1)} async-done(((bf16[2,4096,4,128]{1,3,2,0:T(8,128)(2,1)}), bf16[2,4096,4,128]{1,3,2,0:T(8,128)(2,1)}, u32[]{:S(2)}, u32[]{:S(2)}) %all-to-all-start.4) | async-done | bytes 8388640 | tf_op jit(solution)/shard_map/all_to_all | solution.py:37
  531.3 85.1 %all-to-all-done.2 = bf16[2,4096,4,128]{3,1,2,0:T(8,128)(2,1)} async-done(((bf16[2,4096,4,128]{3,1,2,0:T(8,128)(2,1)}), bf16[2,4096,4,128]{3,1,2,0:T(8,128)(2,1)}, u32[]{:S(2)}, u32[]{:S(2)}) %all-to-all-start.2) | async-done | bytes 8388640 | tf_op jit(solution)/shard_map/all_to_all | solution.py:37
  628.9 48.2 %multiply_convert_fusion = (bf16[4096,4,1024]{2,0,1:T(8,128)(2,1)}, f32[4,4096,1024]{2,1,0:T(8,128)}) fusion(bf16[4,256,1024]{2,1,0:T(8,128)(2,1)S(1)} %copy-done, bf16[4096,4,32,8]{0,2,1,3:T(8,128)(2,1)} %bitcast.188), kind=kOutput, calls=%fused_computation.10 | convolution fusion | flops 8740929536 | bytes 111149056 | tf_op jit(solution)/shard_map/tge,geo->tgo/dot_general | solution.py:25
  677.1 53.2 %fusion.6 = bf16[4096,4,1024]{2,0,1:T(8,128)(2,1)} fusion(f32[4,4096,1024]{2,1,0:T(8,128)} %get-tuple-element.19, bf16[4096,4,256]{0,2,1:T(8,128)(2,1)} %bitcast.186, bf16[4,1024,256]{2,1,0:T(8,128)(2,1)} %param.15), kind=kOutput, calls=%fused_computation.8 | convolution fusion | flops 8908701696 | bytes 111149056 | tf_op jit(solution)/shard_map/tgq,goq->tgo/dot_general | solution.py:25
  730.3 19.0 %convert_bitcast_fusion.3 = bf16[4096,4,256]{0,2,1:T(8,128)(2,1)} fusion(bf16[4096,4,1024]{2,0,1:T(8,128)(2,1)} %fusion.6, bf16[4,256,1024]{2,1,0:T(8,128)(2,1)S(1)} %copy-done), kind=kOutput, calls=%fused_computation.54 | convolution fusion | flops 8594128896 | bytes 44040192 | tf_op jit(solution)/shard_map/tgo,geo->tge/dot_general | solution.py:25
  785.3 103.4 %all_to_all.75 = bf16[2,4096,4,128]{1,3,2,0:T(8,128)(2,1)} all-to-all(bf16[2,4096,4,128]{1,3,2,0:T(8,128)(2,1)} %pad_maximum_fusion.3), channel_id=1, replica_groups=mesh['seq'=16,'fsdp'=2] {'fsdp'}, dimensions={0} | all-to-all | bytes 16777216 | tf_op jit(solution)/shard_map/all_to_all | solution.py:37
  908.0 17.4 %copy.148 = f32[4096,1024]{1,0:T(8,128)} copy(f32[4096,1024]{0,1:T(8,128)} %bitcast.174) | data formatting | bytes 33554432 | tf_op jit(solution)/shard_map/reshape | solution.py:83
  925.5 15.0 fusion.13
  951.8 35.0 %all-to-all-start.6 = ((bf16[16,256,1024]{2,0,1:T(8,128)(2,1)}), bf16[16,256,1024]{2,0,1:T(8,128)(2,1)}, u32[]{:S(2)}, u32[]{:S(2)}) async-start(bf16[16,256,1024]{2,0,1:T(8,128)(2,1)} %copy.149), calls=%async_computation.6 | async-start | bytes 16777216 | tf_op jit(solution)/shard_map/all_to_all | solution.py:30
  986.8 17.1 convert_bitcast_fusion.5
  1015.1 122.2 %all-to-all-done.6 = bf16[16,256,1024]{2,0,1:T(8,128)(2,1)} async-done(((bf16[16,256,1024]{2,0,1:T(8,128)(2,1)}), bf16[16,256,1024]{2,0,1:T(8,128)(2,1)}, u32[]{:S(2)}, u32[]{:S(2)}) %all-to-all-start.6) | async-done | bytes 8388640 | tf_op jit(solution)/shard_map/all_to_all | solution.py:30
  1157.3 23.3 %convert_bitcast_fusion.2 = bf16[256,16,1024]{0,2,1:T(8,128)(2,1)} fusion(bf16[256,16,1024]{2,1,0:T(8,128)(2,1)} %bitcast.172, bf16[256,256]{1,0:T(8,128)(2,1)S(1)} %copy-done.10), kind=kOutput, calls=%fused_computation.53 | convolution fusion | flops 2151677952 | bytes 16908288 | tf_op jit(solution)/shard_map/ajc,ai->ijc/dot_general | solution.py:25
  1193.0 45.2 %all-to-all-done.3 = bf16[2,4096,4,128]{3,1,2,0:T(8,128)(2,1)} async-done(((bf16[2,4096,4,128]{3,1,2,0:T(8,128)(2,1)}), bf16[2,4096,4,128]{3,1,2,0:T(8,128)(2,1)}, u32[]{:S(2)}, u32[]{:S(2)}) %all-to-all-start.3) | async-done | bytes 8388640 | tf_op jit(solution)/shard_map/all_to_all | solution.py:37
  1238.2 36.0 %all-to-all-start.7 = ((bf16[256,16,1024]{2,1,0:T(8,128)(2,1)}), bf16[256,16,1024]{2,1,0:T(8,128)(2,1)}, u32[]{:S(2)}, u32[]{:S(2)}) async-start(bf16[256,16,1024]{2,1,0:T(8,128)(2,1)} %copy.153), calls=%async_computation.7 | async-start | bytes 16777216 | tf_op jit(solution)/shard_map/all_to_all | solution.py:32
  1274.7 20.5 %fusion.51 = f32[4,1024,256]{2,1,0:T(8,128)} fusion(bf16[4096,4,1024]{2,0,1:T(8,128)(2,1)} %get-tuple-element.18, bf16[4096,4,256]{0,2,1:T(8,128)(2,1)} %bitcast.187), kind=kOutput, calls=%fused_computation.83 | convolution fusion | flops 8589934592 | bytes 46137344 | tf_op jit(solution)/shard_map/tgo,tgq->goq/dot_general | solution.py:25
  1295.2 26.2 %fusion.25 = f32[4,256,1024]{2,1,0:T(8,128)} fusion(bf16[4096,4,1024]{2,0,1:T(8,128)(2,1)} %fusion.6, bf16[4096,4,32,8]{0,2,1,3:T(8,128)(2,1)} %bitcast.189), kind=kOutput, calls=%fused_computation.45 | convolution fusion | flops 8589934592 | bytes 46137344 | tf_op jit(solution)/shard_map/tge,tgo->geo/dot_general | solution.py:25
  1355.2 15.4 fusion.23
  1370.5 17.5 %copy.140 = f32[4096,1024]{1,0:T(8,128)} copy(f32[4096,1024]{0,1:T(8,128)} %bitcast.173) | data formatting | bytes 33554432 | tf_op jit(solution)/shard_map/reshape | solution.py:70
  1400.1 248.8 %all-reduce.3.cloned.1.call-done = (f32[4,256,256]{2,1,0:T(8,128)}, f32[4,256,1024]{2,1,0:T(8,128)}, f32[4,1024,256]{2,1,0:T(8,128)}, f32[4,256,256]{2,1,0:T(8,128)}) async-done(((f32[4,256,256]{2,1,0:T(8,128)}, f32[4,256,1024]{2,1,0:T(8,128)}, f32[4,1024,256]{2,1,0:T(8,128)}, f32[4,256,256]{2,1,0:T(8,128)}), (f32[4,256,256]{2,1,0:T(8,128)}, f32[4,256,1024]{2,1,0:T(8,128)}, f32[4,1024,256]{2,1,0:T(8,128)}, ...) | async-done | bytes 10485776 | tf_op jit(solution)/shard_map/psum | solution.py:114
  1688.1 23.6 %fusion.12 = bf16[4096,1024]{1,0:T(8,128)(2,1)} fusion(f32[16,1024,256]{1,2,0:T(8,128)} %fusion.47, f32[16,16,16,1024]{3,2,1,0:T(8,128)} %copy-done.2, bf16[4096,1024]{1,0:T(8,128)(2,1)S(1)} %bitcast.169, f32[4096,1024]{1,0:T(8,128)} %copy.148, bf16[4096,1024]{1,0:T(8,128)(2,1)} %param.17), kind=kLoop, calls=%fused_computation.21 | loop fusion | flops 62914560 | bytes 75497472 | tf_op jit(solution)/shard_map/convert_element_type | solution.py:120
  (82 shorter events, 380.1 us)
Async XLA Ops:
  7.2 621.7 %copy-start = (bf16[4,256,1024]{2,1,0:T(8,128)(2,1)S(1)}, bf16[4,256,1024]{2,1,0:T(8,128)(2,1)}, u32[]{:S(2)}) copy-start(bf16[4,256,1024]{2,1,0:T(8,128)(2,1)} %param.14) | copy-start | bytes 6291460
  217.4 12.9 copy-start.9
  259.4 5.9 copy-start.6
  259.4 156.5 %all-to-all-start.1 = ((bf16[256,16,1024]{2,1,0:T(8,128)(2,1)}), bf16[256,16,1024]{2,1,0:T(8,128)(2,1)}, u32[]{:S(2)}, u32[]{:S(2)}) async-start(bf16[256,16,1024]{2,1,0:T(8,128)(2,1)} %copy.130), calls=%async_computation.1 | async-start | bytes 16777216 | tf_op jit(solution)/shard_map/all_to_all | solution.py:32
  415.8 100.7 %all-to-all-start.4 = ((bf16[2,4096,4,128]{1,3,2,0:T(8,128)(2,1)}), bf16[2,4096,4,128]{1,3,2,0:T(8,128)(2,1)}, u32[]{:S(2)}, u32[]{:S(2)}) async-start(bf16[2,4096,4,128]{1,3,2,0:T(8,128)(2,1)} %pad_maximum_fusion.2), calls=%async_computation.4 | async-start | bytes 16777216 | tf_op jit(solution)/shard_map/all_to_all | solution.py:37
  422.8 24.6 %slice-start = ((s8[8388608]{0:T(1024)(128)(4,1)}), s8[4194304]{0:T(1024)(128)(4,1)S(1)}, s32[]{:S(2)}) async-start(s8[8388608]{0:T(1024)(128)(4,1)} %bitcast.166), calls=%async_computation.9 | async-start | bytes 8388608
  434.4 13.1 slice-start.1
  441.7 5.8 copy-start.2
  456.1 12.0 copy-start.4
  516.5 99.9 %all-to-all-start.2 = ((bf16[2,4096,4,128]{3,1,2,0:T(8,128)(2,1)}), bf16[2,4096,4,128]{3,1,2,0:T(8,128)(2,1)}, u32[]{:S(2)}, u32[]{:S(2)}) async-start(bf16[2,4096,4,128]{3,1,2,0:T(8,128)(2,1)} %pad_maximum_fusion), calls=%async_computation.2 | async-start | bytes 16777216 | tf_op jit(solution)/shard_map/all_to_all | solution.py:37
  888.7 7.8 copy-start.5
  951.8 35.0 %copy-start.12 = (bf16[4,1024,256]{2,1,0:T(8,128)(2,1)S(1)}, bf16[4,1024,256]{2,1,0:T(8,128)(2,1)}, u32[]{:S(2)}) copy-start(bf16[4,1024,256]{2,1,0:T(8,128)(2,1)} %param.15) | copy-start | bytes 6291460
  951.8 185.5 %all-to-all-start.6 = ((bf16[16,256,1024]{2,0,1:T(8,128)(2,1)}), bf16[16,256,1024]{2,0,1:T(8,128)(2,1)}, u32[]{:S(2)}, u32[]{:S(2)}) async-start(bf16[16,256,1024]{2,0,1:T(8,128)(2,1)} %copy.149), calls=%async_computation.6 | async-start | bytes 16777216 | tf_op jit(solution)/shard_map/all_to_all | solution.py:30
  1137.3 100.9 %all-to-all-start.3 = ((bf16[2,4096,4,128]{3,1,2,0:T(8,128)(2,1)}), bf16[2,4096,4,128]{3,1,2,0:T(8,128)(2,1)}, u32[]{:S(2)}, u32[]{:S(2)}) async-start(bf16[2,4096,4,128]{3,1,2,0:T(8,128)(2,1)} %pad_maximum_fusion.1), calls=%async_computation.3 | async-start | bytes 16777216 | tf_op jit(solution)/shard_map/all_to_all | solution.py:37
  1144.5 12.8 copy-start.10
  1238.2 421.4 %all-to-all-start.7 = ((bf16[256,16,1024]{2,1,0:T(8,128)(2,1)}), bf16[256,16,1024]{2,1,0:T(8,128)(2,1)}, u32[]{:S(2)}, u32[]{:S(2)}) async-start(bf16[256,16,1024]{2,1,0:T(8,128)(2,1)} %copy.153), calls=%async_computation.7 | async-start | bytes 16777216 | tf_op jit(solution)/shard_map/all_to_all | solution.py:32
  1274.2 374.7 %all-reduce.3.cloned.1.call-start = ((), (), s32[]{:S(2)}) async-start(), calls=%async_computation.8 | async-start | bytes 20971520 | tf_op jit(solution)/shard_map/psum | solution.py:114
  1354.1 1.0 copy-start.7
  1648.9 8.3 copy-start.3
  1671.0 6.6 copy-start.11
  1677.6 2.4 copy-start.8
  1677.6 10.5 slice-start.2
  1680.0 8.1 slice-start.3
  1688.1 23.6 %copy-start.1 = (bf16[4,256,1024]{2,1,0:T(8,128)(2,1)S(1)}, bf16[4,256,1024]{2,1,0:T(8,128)(2,1)}, u32[]{:S(2)}) copy-start(bf16[4,256,1024]{2,1,0:T(8,128)(2,1)} %param.14) | copy-start | bytes 6291460
Sparse Core Ops, SparseCore 0:
  1354.3 294.6 all-reduce.2
